TPU v7x, 32 devices: a whole 2x2x4 slice. The times are simulated.
32 devices in a mesh: row: 4 (over z), col: 8 (over y, x, core).
Axes of the slice: x: 2, y: 2, z: 4, core: 2. Of those that a mesh axis runs over, the one named last changes fastest.
Arguments:
- dec_src: float32 [2304, 8192], P('col', 'row'), may hold values from -6 to 6
- enc_tgt: float32 [2304, 16384], P('row', 'col'), may hold values from -0.125 to 0.125
- src_coacts: float32 [512, 8192], P('col', 'row'), may hold values from -6 to 6
- tgt_coacts: float32 [512, 16384], P('row', 'col'), may hold values from -6 to 6
- eval_src: float32 [512, 8192], P('col', 'row'), may hold values from -6 to 6
- enc_bias: float32 [16384], P('col'), may hold values from -0.5 to 0.5
- dec_tgt: float32 [2304, 16384], P('row', 'col'), may hold values from -0.046875 to 0.046875
- tile_mask: int32 [128, 256], P('row', 'col'), may hold values from 0 to 1, as said below
Outputs:
- recon: float32 [512, 2304], P('col', 'row')
Inputs may be any that keep to these rules, and one draw needn't show every extreme that they name: `tile_mask`: 1 keeps a tile, 0 prunes it; the share of kept tiles differs between regions of the grid.
All inputs are finite; a program needn't handle non-finite values.
Results may differ from a plain program's by a relative error of at most 0.0003.
Values sent between devices are 32-bit elements; how exact they have to be, the bound alone decides.
A program may use at most 192 MiB of HBM per device.

v0:
```python
import functools

import jax
import jax.numpy as jnp
from jax import lax
from jax.experimental import pallas as pl
from jax.experimental.pallas import tpu as pltpu
from jax.sharding import PartitionSpec as P


CHUNKS = 2


def split(value):
    high = value.astype(jnp.bfloat16)
    return high, (value - high.astype(jnp.float32)).astype(jnp.bfloat16)


def dot3(left, rows, right, left_dim, right_dim):
    def one(a, b):
        return lax.dot_general(a, b, (((left_dim,), (right_dim,)), ((), ())), preferred_element_type=jnp.float32)

    both = one(left, right[0])
    return both[:rows] + (both[rows:] + one(left[:rows], right[1]))


def prepare(enc_rows, row, *refs):
    blocks, (enc_both, tgt_both, ordered) = refs[:-3], refs[-3:]
    n_row, height = len(blocks), ordered.shape[2]
    for step, block in enumerate(blocks):
        ordered[lax.rem(row[0] + n_row - step, n_row)] = block[...]
    for rows, out in ((slice(None, enc_rows), enc_both), (slice(enc_rows, None), tgt_both)):
        out[:height], out[height:] = split(ordered[:, rows, :].reshape(-1, height).T)


def prepare_target(row, blocks, enc_rows):
    n_row = len(blocks)
    rows, height = blocks[0].shape
    shapes = [(2 * height, n_row * n) for n in (enc_rows, rows - enc_rows)]
    return pl.pallas_call(
        functools.partial(prepare, enc_rows),
        in_specs=[pl.BlockSpec(memory_space=pltpu.SMEM)] + [pl.BlockSpec(memory_space=pltpu.VMEM)] * n_row,
        out_specs=[pl.BlockSpec(memory_space=pltpu.VMEM)] * 2,
        out_shape=[jax.ShapeDtypeStruct(shape, jnp.bfloat16) for shape in shapes],
        scratch_shapes=[pltpu.VMEM((n_row, rows, height), jnp.float32)],
        compiler_params=pltpu.CompilerParams(vmem_limit_bytes=60 * 1024 * 1024),
        cost_estimate=pl.CostEstimate(flops=0, bytes_accessed=8 * n_row * rows * height, transcendentals=0),
    )(row.reshape(1), *blocks)


def weigh(dec_rows, src_rows, norm, source, enc_both, tgt_both, mask, out):
    width = source.shape[2]
    height = out.shape[0]

    @pl.when(pl.program_id(0) == 0)
    def _():
        out[...] = jnp.zeros_like(out)

    dec = split(source[:, :dec_rows, :].reshape(-1, width))
    virtual = dot3(enc_both[...], height, dec, 1, 0)
    src = split(source[:, dec_rows : dec_rows + src_rows, :].reshape(-1, width))
    coact = dot3(tgt_both[...], height, src, 1, 0) * norm
    tiles = mask.shape[1]
    keep = jnp.broadcast_to(mask[0][:, None, :], (tiles, height // tiles, width)).reshape(height, width)
    weighted = jnp.concatenate(split(virtual * coact * keep), axis=0)
    evals = split(source[:, dec_rows + src_rows :, :].reshape(-1, width))
    out[...] += dot3(weighted, height, evals, 1, 1)


def partial_pre(source, target, mask, dec_rows, src_rows, norm):
    n_col, packed, count = source.shape
    height = target[0].shape[0] // 2
    depth, stats = target[0].shape[1], target[1].shape[1]
    width = min(256, count)
    evals = n_col * (packed - dec_rows - src_rows)
    return pl.pallas_call(
        functools.partial(weigh, dec_rows, src_rows, norm),
        grid=(count // width,),
        in_specs=[
            pl.BlockSpec((n_col, packed, width), lambda i: (0, 0, i)),
            pl.BlockSpec(target[0].shape, lambda i: (0, 0)),
            pl.BlockSpec(target[1].shape, lambda i: (0, 0)),
            pl.BlockSpec((1, mask.shape[1], width), lambda i: (0, 0, i)),
        ],
        out_specs=pl.BlockSpec((height, evals), lambda i: (0, 0)),
        out_shape=jax.ShapeDtypeStruct((height, evals), jnp.float32),
        compiler_params=pltpu.CompilerParams(vmem_limit_bytes=60 * 1024 * 1024),
        cost_estimate=pl.CostEstimate(
            flops=6 * count * height * (depth + stats + evals),
            bytes_accessed=4 * (source.size + height * (depth + stats)),
            transcendentals=0,
        ),
    )(source, *target, mask)


def layer(n_row, dec_src, enc_tgt, src_coacts, tgt_coacts, eval_src, enc_bias, dec_tgt, tile_mask):
    members = n_row // 2
    src_count = dec_src.shape[1]
    half = enc_tgt.shape[1] // 2
    chunk = half // CHUNKS
    piece = chunk // members
    dec_rows, src_rows, enc_rows = dec_src.shape[0], src_coacts.shape[0], enc_tgt.shape[0]
    stats = tgt_coacts.shape[0] * n_row
    tile = src_count // tile_mask.shape[0]
    row = lax.axis_index("row")
    parity = lax.rem(row, 2)
    group = row // 2
    norm = 1.0 / float(stats) ** 0.5

    packed = jnp.concatenate([dec_src, src_coacts, eval_src], axis=0)
    packed_other = lax.ppermute(packed, "row", [(r, r ^ 1) for r in range(n_row)])
    mask_t = tile_mask.T.astype(jnp.float32)
    mask_here = lax.dynamic_slice_in_dim(mask_t, parity * (half // tile), half // tile, 0)
    mask_there = lax.dynamic_slice_in_dim(mask_t, (1 - parity) * (half // tile), half // tile, 0)
    mask_other = lax.ppermute(mask_there, "row", [(r, r ^ 1) for r in range(n_row)])

    sources = [(lax.all_gather(packed, "col", axis=0, tiled=False), jnp.repeat(mask_here, tile, axis=1))]
    gathered = lax.all_gather(packed_other, "col", axis=0, tiled=False)
    sources.append((gathered, jnp.repeat(mask_other, tile, axis=1)))

    targets = []
    for k in range(CHUNKS):
        def columns(side):
            start = side * half + k * chunk
            return jnp.concatenate(
                [lax.dynamic_slice_in_dim(a, start, chunk, 1) for a in (enc_tgt, tgt_coacts)], axis=0
            )

        same, across = columns(parity), columns(1 - parity)
        blocks = []
        for step in range(n_row):
            block = same if step % 2 == 0 else across
            if step:
                block = lax.ppermute(block, "row", [(r, (r + step) % n_row) for r in range(n_row)])
            blocks.append(block)
        targets.append(prepare_target(row, blocks, enc_rows))

    scale = 1.0 / jnp.sqrt(jnp.float32(src_count * n_row))
    recon_part = None
    for k in range(CHUNKS):
        partial = None
        for gathered, mask in sources:
            rows = chunk // tile
            term = partial_pre(gathered, targets[k], mask[None, k * rows : (k + 1) * rows], dec_rows, src_rows, norm)
            partial = term if partial is None else partial + term
        total = lax.dynamic_slice_in_dim(partial, group * piece, piece, 0)
        for step in range(1, members):
            target = lax.rem(group + step, members)
            sent = lax.dynamic_slice_in_dim(partial, target * piece, piece, 0)
            arrived = lax.ppermute(sent, "row", [(r, (r + 2 * step) % n_row) for r in range(n_row)])
            total = total + arrived
        bias = lax.dynamic_slice_in_dim(enc_bias, parity * half + k * chunk + group * piece, piece, 0)
        hidden = jnp.maximum(total * scale + bias[:, None], 0.0)
        hidden_all = lax.all_gather(hidden, "row", axis=0, tiled=True)
        starts = [(r % 2) * half + k * chunk + (r // 2) * piece for r in range(n_row)]
        dec_part = jnp.concatenate([dec_tgt[:, s : s + piece] for s in starts], axis=1)
        term = lax.dot_general(
            hidden_all, dec_part, (((0,), (1,)), ((), ())),
            precision=lax.Precision.HIGH, preferred_element_type=jnp.float32,
        )
        recon_part = term if recon_part is None else recon_part + term
    return lax.psum_scatter(recon_part, "col", scatter_dimension=0, tiled=True)


MESH = pl.DeviceIdType.MESH
T_CHUNKS = 4
S_CHUNKS = 4
X, Y, CORE = 2, 4, 1
HOPS = (
    (0, "all", X), (0, "all", Y), (0, "all", CORE),
    (X, "all", CORE), (Y, "all", CORE),
    (X, "top", Y), (Y, "low", X),
    (X ^ Y, "top", CORE), (X ^ Y, "low", CORE),
)


def fused(sizes, packed, blocks, masks, bias, dec_tgt, out, sbuf, tbuf, *scratch):
    n_row, n_col, dec_rows, src_rows, enc_rows, norm, scale = sizes
    (tstage, encs, tgts, stage, mask, acc, arrived, hidden, decoder, recon, rsend, rrecv,
     t_send, t_recv, s_send, s_recv, m_send, m_recv, x_send, x_recv, p_send, p_recv, h_send, h_recv,
     r_send, r_recv, local_sem, load_sem) = scratch
    r, c = lax.axis_index("row"), lax.axis_index("col")
    parity = lax.rem(r, 2)
    count = packed.shape[1]
    jw = count // S_CHUNKS
    half = blocks.shape[1] // 2
    w = half // T_CHUNKS
    packed_rows = packed.shape[0]
    width = min(256, jw)

    def row_of(step):
        return lax.rem(r + step, n_row)

    def remote(src, dst, send, recv, row, col):
        return pltpu.make_async_remote_copy(
            src_ref=src, dst_ref=dst, send_sem=send, recv_sem=recv, device_id=(row, col), device_id_type=MESH
        )

    def t_cols(side, k):
        return pl.ds(pl.multiple_of(side * half + k * w, w), w)

    def t_copy(k, step):
        to = row_of(step)
        return remote(
            blocks.at[:, t_cols(lax.rem(to, 2), k)], tbuf.at[k, r], t_send.at[k, step - 1], t_recv.at[k, step - 1], to, c
        )

    def t_wait(k, step):
        slot = tbuf.at[k, row_of(n_row - step)]
        remote(slot, slot, t_send.at[k, step - 1], t_recv.at[k, step - 1], row_of(step), c).wait_recv()

    def s_cols(j):
        return pl.ds(pl.multiple_of(j * jw, jw), jw)

    def s_copy(j):
        return remote(packed.at[:, s_cols(j)], sbuf.at[1, c, :, s_cols(j)], s_send.at[j], s_recv.at[j], r ^ 1, c)

    def m_copy():
        return remote(masks.at[1 - parity], mask.at[1], m_send, m_recv, r ^ 1, c)

    parts = {
        "all": pl.ds(0, packed_rows),
        "top": pl.ds(0, packed_rows // 2),
        "low": pl.ds(packed_rows // 2, packed_rows - packed_rows // 2),
    }

    def hop(q, n):
        whose, rows, to = HOPS[n]
        block, j = q // S_CHUNKS, q % S_CHUNKS
        dst = sbuf.at[block, c ^ whose, parts[rows], s_cols(j)]
        src = packed.at[parts[rows], s_cols(j)] if whose == 0 and block == 0 else dst
        return remote(src, dst, x_send.at[q, n], x_recv.at[q, n], r, c ^ to)

    def hop_wait(q, n):
        whose, rows, to = HOPS[n]
        block, j = q // S_CHUNKS, q % S_CHUNKS
        dst = sbuf.at[block, c ^ whose ^ to, parts[rows], s_cols(j)]
        remote(dst, dst, x_send.at[q, n], x_recv.at[q, n], r, c ^ to).wait_recv()

    chunks = 2 * S_CHUNKS

    def spread(q):
        if q >= S_CHUNKS:
            s_copy(q - S_CHUNKS).wait_recv()
        for n in (0, 1, 2):
            hop(q, n).start()

    def step(q):
        if q < chunks:
            hop_wait(q, 0)
            hop(q, 5).start()
            hop(q, 3).start()
            hop_wait(q, 1)
            hop(q, 6).start()
            hop(q, 4).start()
        if q + 2 < chunks:
            spread(q + 2)
        if q >= 1:
            hop_wait(q - 1, 5)
            hop(q - 1, 7).start()
            hop_wait(q - 1, 6)
            hop(q - 1, 8).start()

    def landed(q):
        for n in (2, 3, 4, 7, 8):
            hop_wait(q, n)

    def load_copies(block, j, slot):
        copies = []
        for i in range(n_col):
            s = c ^ i
            copies.append(
                pltpu.make_async_copy(sbuf.at[block, s, :, s_cols(j)], stage.at[slot, s], load_sem.at[slot, i])
            )
        own = pltpu.make_async_copy(packed.at[:, s_cols(j)], stage.at[slot, c], load_sem.at[slot, 0])
        return copies, own

    def load_start(block, j, slot):
        copies, own = load_copies(block, j, slot)

        @pl.when(block == 0)
        def _():
            own.start()

        @pl.when(block != 0)
        def _():
            copies[0].start()

        for copy in copies[1:]:
            copy.start()

    def load_wait(slot):
        for i in range(n_col):
            s = c ^ i
            pltpu.make_async_copy(packed.at[:, s_cols(0)], stage.at[slot, s], load_sem.at[slot, i]).wait()

    def prepare_chunk(k):
        for s in range(1, n_row):
            t_wait(k, s)
        own = pltpu.make_async_copy(blocks.at[:, t_cols(parity, k)], tstage.at[r], local_sem.at[0])
        others = [
            pltpu.make_async_copy(tbuf.at[k, row_of(s)], tstage.at[row_of(s)], local_sem.at[s]) for s in range(1, n_row)
        ]
        for copy in [own] + others:
            copy.start()
        for copy in [own] + others:
            copy.wait()
        for rows, into in ((slice(None, enc_rows), encs), (slice(enc_rows, None), tgts)):
            into[k, :w], into[k, w:] = split(tstage[:, rows, :].reshape(-1, w).T)

    def compute(k, block, j, slot):
        @pl.loop(0, jw // width)
        def _(i):
            lanes = pl.ds(pl.multiple_of(i * width, width), width)
            dec = split(stage[slot, :, :dec_rows, lanes].reshape(-1, width))
            virtual = dot3(encs[k], w, dec, 1, 0)
            src = split(stage[slot, :, dec_rows : dec_rows + src_rows, lanes].reshape(-1, width))
            coact = dot3(tgts[k], w, src, 1, 0) * norm
            keep = mask[block, k, :, pl.ds(pl.multiple_of(j * jw + i * width, width), width)]
            tiles = keep.shape[0]
            keep = jnp.broadcast_to(keep[:, None, :], (tiles, w // tiles, width)).reshape(w, width)
            weighted = jnp.concatenate(split(virtual * coact * keep), axis=0)
            evals = split(stage[slot, :, dec_rows + src_rows :, lanes].reshape(-1, width))
            acc[k] += dot3(weighted, w, evals, 1, 1)

    def p_copy(k):
        return remote(acc.at[k], arrived.at[k], p_send.at[k], p_recv.at[k], r ^ 2, c)

    def h_copy(k, side):
        return remote(hidden.at[side, k], hidden.at[side, k], h_send.at[k], h_recv.at[k], r ^ 1, c)

    def activate(k):
        p_copy(k).wait_recv()
        column = bias[pl.ds(pl.multiple_of(parity * half + k * w, w), w), :]
        hidden[parity, k] = jnp.maximum((acc[k] + arrived[k]) * scale + column, 0.0)
        h_copy(k, parity).start()

    def decode(k):
        h_copy(k, 1 - parity).wait_recv()
        for side in range(2):
            left = jnp.concatenate(split(decoder[:, t_cols(side, k)]), axis=0)
            recon[...] += dot3(left, decoder.shape[0], split(hidden[side, k]), 1, 0)

    def scatter_copy(i):
        rows = rsend.shape[0] // n_col
        there = c ^ i
        return remote(
            rsend.at[pl.ds(pl.multiple_of(there * rows, rows), rows)], rrecv.at[c], r_send.at[i - 1], r_recv.at[i - 1], r, there
        )

    def scatter_wait(i):
        remote(rrecv.at[c ^ i], rrecv.at[c ^ i], r_send.at[i - 1], r_recv.at[i - 1], r, c ^ i).wait_recv()

    barrier = pltpu.get_barrier_semaphore()
    for s in range(1, n_row):
        pl.semaphore_signal(barrier, inc=1, device_id=(row_of(s), c), device_id_type=MESH)
    for i in range(1, n_col):
        pl.semaphore_signal(barrier, inc=1, device_id=(r, c ^ i), device_id_type=MESH)
    pl.semaphore_wait(barrier, n_row + n_col - 2)

    m_copy().start()
    for s in range(1, n_row):
        t_copy(0, s).start()
    spread(0)
    for j in range(S_CHUNKS):
        s_copy(j).start()
    spread(1)
    for k in range(1, T_CHUNKS):
        for s in range(1, n_row):
            t_copy(k, s).start()
    own_mask = pltpu.make_async_copy(masks.at[parity], mask.at[0], local_sem.at[n_row])
    own_mask.start()
    own_decoder = pltpu.make_async_copy(dec_tgt, decoder, local_sem.at[n_row + 1])
    own_decoder.start()
    acc[...] = jnp.zeros_like(acc)
    recon[...] = jnp.zeros_like(recon)
    step(0)
    step(1)
    own_mask.wait()
    own_decoder.wait()
    m_copy().wait_recv()

    def where(g):
        k = jnp.where(g < 6, 0, jnp.where(g < 12, 1, jnp.where(g < 16, g % 2, g // 8)))
        block = jnp.where(
            g < 4, 0, jnp.where(g < 6, 1, jnp.where(g < 10, 0, jnp.where(g < 16, 1, (g // 4) % 2)))
        )
        j = jnp.where(
            g < 4, g, jnp.where(g < 6, g - 4, jnp.where(g < 10, g - 6, jnp.where(g < 12, g - 10, jnp.where(g < 16, 2 + (g - 12) // 2, g % 4))))
        )
        return k, block, j

    needs = {0: 0, 1: 1, 2: 2, 3: 3, 4: 4, 5: 5, 12: 6, 14: 7}
    steps = {1: 2, 2: 3, 3: 4, 4: 5, 5: 6, 12: 7, 14: 8}

    @pl.loop(0, T_CHUNKS * chunks)
    def _(g):
        k, block, j = where(g)
        slot = g % 2
        for at, q in needs.items():
            @pl.when(g == at)
            def _(at=at, q=q):
                if at in steps:
                    step(steps[at])
                landed(q)

        waits = functools.reduce(jnp.logical_or, [g == at for at in needs])
        next_waits = functools.reduce(jnp.logical_or, [g + 1 == at for at in needs])

        @pl.when(waits)
        def _():
            load_start(block, j, slot)

        @pl.when((g == 0) | (g == 6) | (g == 16) | (g == 24))
        def _():
            prepare_chunk(k)

        @pl.when(jnp.logical_not(next_waits) & (g + 1 < T_CHUNKS * chunks))
        def _():
            load_start(*where(g + 1)[1:], 1 - slot)

        load_wait(slot)
        compute(k, block, j, slot)

        @pl.when((g == 14) | (g == 15) | (g == 23) | (g == 31))
        def _():
            p_copy(k).start()

        @pl.when((g == 27) | (g == 28) | (g == 30))
        def _():
            activate(jnp.where(g == 30, 2, g - 27))

    for k in range(T_CHUNKS):
        if k == T_CHUNKS - 1:
            activate(k)
        decode(k)
    rsend[...] = recon[...].T
    for i in range(1, n_col):
        scatter_copy(i).start()
    rows = rsend.shape[0] // n_col
    for i in range(1, n_col):
        scatter_wait(i)
    total = rsend[pl.ds(pl.multiple_of(c * rows, rows), rows), :]
    for i in range(1, n_col):
        total = total + rrecv[c ^ i]
    out[...] = total

    m_copy().wait_send()
    for j in range(S_CHUNKS):
        s_copy(j).wait_send()
    for k in range(T_CHUNKS):
        for s in range(1, n_row):
            t_copy(k, s).wait_send()
        p_copy(k).wait_send()
        h_copy(k, parity).wait_send()
    for q in range(chunks):
        for n in range(len(HOPS)):
            hop(q, n).wait_send()
    for i in range(1, n_col):
        scatter_copy(i).wait_send()


def whole(n_row, n_col, dec_src, enc_tgt, src_coacts, tgt_coacts, eval_src, enc_bias, dec_tgt, tile_mask):
    count, features = dec_src.shape[1], enc_tgt.shape[1]
    dec_rows, src_rows, ev_rows = dec_src.shape[0], src_coacts.shape[0], eval_src.shape[0]
    enc_rows, tgt_rows = enc_tgt.shape[0], tgt_coacts.shape[0]
    half = features // 2
    w = half // T_CHUNKS
    jw = count // S_CHUNKS
    packed = jnp.concatenate([dec_src, src_coacts, eval_src], axis=0)
    blocks = jnp.concatenate([enc_tgt, tgt_coacts], axis=0)
    tile = count // tile_mask.shape[0]
    masks = jnp.repeat(tile_mask.T.astype(jnp.float32), tile, axis=1).reshape(2, T_CHUNKS, w // tile, count)
    sizes = (
        n_row, n_col, dec_rows, src_rows, enc_rows,
        1.0 / float(tgt_rows * n_row) ** 0.5, 1.0 / float(count * n_row) ** 0.5,
    )
    evals = ev_rows * n_col
    depth, stats = dec_rows * n_col, src_rows * n_col
    anywhere, vmem = pl.BlockSpec(memory_space=pl.ANY), pl.BlockSpec(memory_space=pltpu.VMEM)
    dma = pltpu.SemaphoreType.DMA
    f32, bf16 = jnp.float32, jnp.bfloat16
    hops = (2 * S_CHUNKS, len(HOPS))
    outs = pl.pallas_call(
        functools.partial(fused, sizes),
        in_specs=[anywhere, anywhere, anywhere, vmem, anywhere],
        out_specs=[vmem, anywhere, anywhere],
        out_shape=[
            jax.ShapeDtypeStruct((ev_rows, dec_tgt.shape[0]), f32),
            jax.ShapeDtypeStruct((2, n_col, packed.shape[0], count), f32),
            jax.ShapeDtypeStruct((T_CHUNKS, n_row, blocks.shape[0], w), f32),
        ],
        scratch_shapes=[
            pltpu.VMEM((n_row, blocks.shape[0], w), f32),
            pltpu.VMEM((T_CHUNKS, 2 * w, depth), bf16),
            pltpu.VMEM((T_CHUNKS, 2 * w, stats), bf16),
            pltpu.VMEM((2, n_col, packed.shape[0], jw), f32),
            pltpu.VMEM((2,) + masks.shape[1:], f32),
            pltpu.VMEM((T_CHUNKS, w, evals), f32),
            pltpu.VMEM((T_CHUNKS, w, evals), f32),
            pltpu.VMEM((2, T_CHUNKS, w, evals), f32),
            pltpu.VMEM(dec_tgt.shape, f32),
            pltpu.VMEM((dec_tgt.shape[0], evals), f32),
            pltpu.VMEM((evals, dec_tgt.shape[0]), f32),
            pltpu.VMEM((n_col, ev_rows, dec_tgt.shape[0]), f32),
            dma((T_CHUNKS, n_row - 1)), dma((T_CHUNKS, n_row - 1)),
            dma((S_CHUNKS,)), dma((S_CHUNKS,)),
            dma(()), dma(()),
            dma(hops), dma(hops),
            dma((T_CHUNKS,)), dma((T_CHUNKS,)),
            dma((T_CHUNKS,)), dma((T_CHUNKS,)),
            dma((n_col - 1,)), dma((n_col - 1,)),
            dma((n_row + 2,)), dma((2, n_col)),
        ],
        compiler_params=pltpu.CompilerParams(
            collective_id=0, has_side_effects=True, vmem_limit_bytes=VMEM_LIMIT
        ),
    )(packed, blocks, masks, enc_bias.reshape(-1, 1), dec_tgt)
    return outs[0]


VMEM_LIMIT = 67000000


def solution(mesh):
    n_row, n_col = mesh.shape["row"], mesh.shape["col"]
    if (n_row, n_col) == (4, 8):
        return jax.shard_map(
            functools.partial(whole, n_row, n_col), mesh=mesh, in_specs=SPECS, out_specs=P("col", "row"), check_vma=False
        )
    return stepwise(mesh)


SPECS = (
    P("col", "row"), P("row", "col"), P("col", "row"), P("row", "col"),
    P("col", "row"), P("col"), P("row", "col"), P("row", "col"),
)


def stepwise(mesh):
    return jax.shard_map(
        functools.partial(layer, mesh.shape["row"]),
        mesh=mesh,
        in_specs=(
            P("col", "row"),
            P("row", "col"),
            P("col", "row"),
            P("row", "col"),
            P("col", "row"),
            P("col"),
            P("row", "col"),
            P("row", "col"),
        ),
        out_specs=P("col", "row"),
        check_vma=False,
    )
```

profile of v0, /device:TPU:9, one launch (start us, length us, event | category | flops | bytes accessed | tf_op | source)
XLA Modules:
  0.0 436.0 jit_solution(18135393649591954446)
XLA Ops:
  0.0 0.0 copy-start.1
  0.0 0.8 convert_bitcast_fusion
  0.8 0.1 copy.10
  0.9 0.2 broadcast_in_dim.3
  1.1 0.9 reshape_reshape.3.masks
  2.0 2.1 copy.11.bias
  4.1 0.0 copy-start
  4.1 4.2 pad_maximum_fusion.1.packed
  8.4 0.0 copy-done.1
  8.4 0.0 copy-done
  8.4 3.1 pad_maximum_fusion.blocks
  11.5 422.9 %shard_map.82 = (f32[64,576]{1,0:T(8,128)}, f32[2,8,416,2048]{3,2,1,0:T(8,128)}, f32[4,4,704,256]{3,2,1,0:T(8,128)}) custom-call(f32[416,2048]{1,0:T(8,128)} %pad_maximum_fusion.1.packed, f32[704,2048]{1,0:T(8,128)} %pad_maximum_fusion.blocks, f32[2,4,4,2048]{3,2,1,0:T(4,128)} %reshape_reshape.3.masks, f32[2048,1]{1,0:T(8,128)} %copy.11.bias, ...), custom_call_target="tpu_custom_call" | custom-call | tf_op jit(solution)/shard_map/pallas_call | solution.py:484
  434.4 1.6 copy.13
Async XLA Ops:
  0.0 8.4 %copy-start.1 = (f32[128,2048]{1,0:T(8,128)S(1)}, f32[128,2048]{1,0:T(8,128)}, u32[]{:S(2)}) copy-start(f32[128,2048]{1,0:T(8,128)} %param.11) | copy-start | bytes 3145732
  4.1 4.2 copy-start
where the time goes:
time: 436 us
  Pallas kernels  423 us (97%)
  other arithmetic  8.2 us (2%)
  local copies, waits for them, and re-layouts  4.9 us (1%)
    pallas_call x1, Pallas kernels, whole(): pl.pallas_call(functools.partial(fused, sizes), in_specs=[anywhere, anywh...  423 us

commit v1 on v0

--- a/solution.py
+++ b/solution.py
@@ -174,19 +174,18 @@
 )
 
 
-def fused(sizes, packed, blocks, masks, bias, dec_tgt, out, sbuf, tbuf, *scratch):
+def fused(sizes, dec_src, src_coacts, eval_src, enc_tgt, tgt_coacts, masks, bias, dec_tgt, out, sbuf, tbuf, *scratch):
     n_row, n_col, dec_rows, src_rows, enc_rows, norm, scale = sizes
-    (tstage, encs, tgts, stage, mask, acc, arrived, hidden, decoder, recon, rsend, rrecv,
+    (tstage, encs, tgts, stage, mask, acc, arrived, hidden, decoder, recon, rsend, rrecv, rsum, rlast,
      t_send, t_recv, s_send, s_recv, m_send, m_recv, x_send, x_recv, p_send, p_recv, h_send, h_recv,
      r_send, r_recv, local_sem, load_sem) = scratch
     r, c = lax.axis_index("row"), lax.axis_index("col")
     parity = lax.rem(r, 2)
-    count = packed.shape[1]
+    count = dec_src.shape[1]
     jw = count // S_CHUNKS
-    half = blocks.shape[1] // 2
+    half = enc_tgt.shape[1] // 2
     w = half // T_CHUNKS
-    packed_rows = packed.shape[0]
-    width = min(256, jw)
+    packed_rows = dec_rows + src_rows + eval_src.shape[0]
 
     def row_of(step):
         return lax.rem(r + step, n_row)
@@ -199,21 +198,38 @@
     def t_cols(side, k):
         return pl.ds(pl.multiple_of(side * half + k * w, w), w)
 
-    def t_copy(k, step):
+    def t_start(k, step):
         to = row_of(step)
-        return remote(
-            blocks.at[:, t_cols(lax.rem(to, 2), k)], tbuf.at[k, r], t_send.at[k, step - 1], t_recv.at[k, step - 1], to, c
-        )
-
-    def t_wait(k, step):
+        start = 0
+        for a in (enc_tgt, tgt_coacts):
+            rows = pl.ds(start, a.shape[0])
+            start += a.shape[0]
+            remote(
+                a.at[:, t_cols(lax.rem(to, 2), k)], tbuf.at[k, r, rows],
+                t_send.at[k, step - 1], t_recv.at[k, step - 1], to, c,
+            ).start()
+
+    def t_whole(k, step):
         slot = tbuf.at[k, row_of(n_row - step)]
-        remote(slot, slot, t_send.at[k, step - 1], t_recv.at[k, step - 1], row_of(step), c).wait_recv()
+        return remote(slot, slot, t_send.at[k, step - 1], t_recv.at[k, step - 1], row_of(step), c)
 
     def s_cols(j):
         return pl.ds(pl.multiple_of(j * jw, jw), jw)
 
+    def packed(j, dst):
+        start = 0
+        for a in (dec_src, src_coacts, eval_src):
+            rows = pl.ds(start, a.shape[0])
+            start += a.shape[0]
+            yield a.at[:, s_cols(j)], dst(rows)
+
+    def s_start(j):
+        for src, dst in packed(j, lambda rows: sbuf.at[1, c, rows, s_cols(j)]):
+            remote(src, dst, s_send.at[j], s_recv.at[j], r ^ 1, c).start()
+
     def s_copy(j):
-        return remote(packed.at[:, s_cols(j)], sbuf.at[1, c, :, s_cols(j)], s_send.at[j], s_recv.at[j], r ^ 1, c)
+        whole_chunk = sbuf.at[1, c, :, s_cols(j)]
+        return remote(whole_chunk, whole_chunk, s_send.at[j], s_recv.at[j], r ^ 1, c)
 
     def m_copy():
         return remote(masks.at[1 - parity], mask.at[1], m_send, m_recv, r ^ 1, c)
@@ -228,8 +244,7 @@
         whose, rows, to = HOPS[n]
         block, j = q // S_CHUNKS, q % S_CHUNKS
         dst = sbuf.at[block, c ^ whose, parts[rows], s_cols(j)]
-        src = packed.at[parts[rows], s_cols(j)] if whose == 0 and block == 0 else dst
-        return remote(src, dst, x_send.at[q, n], x_recv.at[q, n], r, c ^ to)
+        return remote(dst, dst, x_send.at[q, n], x_recv.at[q, n], r, c ^ to)
 
     def hop_wait(q, n):
         whose, rows, to = HOPS[n]
@@ -243,7 +258,11 @@
         if q >= S_CHUNKS:
             s_copy(q - S_CHUNKS).wait_recv()
         for n in (0, 1, 2):
-            hop(q, n).start()
+            if q >= S_CHUNKS:
+                hop(q, n).start()
+            else:
+                for src, dst in packed(q, lambda rows: sbuf.at[0, c, rows, s_cols(q)]):
+                    remote(src, dst, x_send.at[q, n], x_recv.at[q, n], r, c ^ HOPS[n][2]).start()
 
     def step(q):
         if q < chunks:
@@ -265,63 +284,56 @@
         for n in (2, 3, 4, 7, 8):
             hop_wait(q, n)
 
-    def load_copies(block, j, slot):
-        copies = []
+    def load(block, j, slot, i):
+        s = c ^ i
+        return pltpu.make_async_copy(sbuf.at[block, s, :, s_cols(j)], stage.at[slot, s], load_sem.at[slot, i])
+
+    def load_start(block, j, slot):
+        @pl.when(block == 0)
+        def _():
+            for src, dst in packed(j, lambda rows: stage.at[slot, c, rows]):
+                pltpu.make_async_copy(src, dst, load_sem.at[slot, 0]).start()
+
+        @pl.when(block != 0)
+        def _():
+            load(block, j, slot, 0).start()
+
+        for i in range(1, n_col):
+            load(block, j, slot, i).start()
+
+    def load_wait(slot):
         for i in range(n_col):
-            s = c ^ i
-            copies.append(
-                pltpu.make_async_copy(sbuf.at[block, s, :, s_cols(j)], stage.at[slot, s], load_sem.at[slot, i])
-            )
-        own = pltpu.make_async_copy(packed.at[:, s_cols(j)], stage.at[slot, c], load_sem.at[slot, 0])
-        return copies, own
-
-    def load_start(block, j, slot):
-        copies, own = load_copies(block, j, slot)
-
-        @pl.when(block == 0)
-        def _():
-            own.start()
-
-        @pl.when(block != 0)
-        def _():
-            copies[0].start()
-
+            load(0, 0, slot, i).wait()
+
+    def prepare_chunk(k):
+        for s in range(1, n_row):
+            t_whole(k, s).wait_recv()
+        start = 0
+        for a in (enc_tgt, tgt_coacts):
+            rows = pl.ds(start, a.shape[0])
+            start += a.shape[0]
+            pltpu.make_async_copy(a.at[:, t_cols(parity, k)], tstage.at[r, rows], local_sem.at[0]).start()
+        copies = [
+            pltpu.make_async_copy(tbuf.at[k, row_of(s)], tstage.at[row_of(s)], local_sem.at[s]) for s in range(n_row)
+        ]
         for copy in copies[1:]:
             copy.start()
-
-    def load_wait(slot):
-        for i in range(n_col):
-            s = c ^ i
-            pltpu.make_async_copy(packed.at[:, s_cols(0)], stage.at[slot, s], load_sem.at[slot, i]).wait()
-
-    def prepare_chunk(k):
-        for s in range(1, n_row):
-            t_wait(k, s)
-        own = pltpu.make_async_copy(blocks.at[:, t_cols(parity, k)], tstage.at[r], local_sem.at[0])
-        others = [
-            pltpu.make_async_copy(tbuf.at[k, row_of(s)], tstage.at[row_of(s)], local_sem.at[s]) for s in range(1, n_row)
-        ]
-        for copy in [own] + others:
-            copy.start()
-        for copy in [own] + others:
+        for copy in copies:
             copy.wait()
         for rows, into in ((slice(None, enc_rows), encs), (slice(enc_rows, None), tgts)):
             into[k, :w], into[k, w:] = split(tstage[:, rows, :].reshape(-1, w).T)
 
     def compute(k, block, j, slot):
-        @pl.loop(0, jw // width)
-        def _(i):
-            lanes = pl.ds(pl.multiple_of(i * width, width), width)
-            dec = split(stage[slot, :, :dec_rows, lanes].reshape(-1, width))
-            virtual = dot3(encs[k], w, dec, 1, 0)
-            src = split(stage[slot, :, dec_rows : dec_rows + src_rows, lanes].reshape(-1, width))
-            coact = dot3(tgts[k], w, src, 1, 0) * norm
-            keep = mask[block, k, :, pl.ds(pl.multiple_of(j * jw + i * width, width), width)]
-            tiles = keep.shape[0]
-            keep = jnp.broadcast_to(keep[:, None, :], (tiles, w // tiles, width)).reshape(w, width)
-            weighted = jnp.concatenate(split(virtual * coact * keep), axis=0)
-            evals = split(stage[slot, :, dec_rows + src_rows :, lanes].reshape(-1, width))
-            acc[k] += dot3(weighted, w, evals, 1, 1)
+        dec = split(stage[slot, :, :dec_rows, :].reshape(-1, jw))
+        virtual = dot3(encs[k], w, dec, 1, 0)
+        src = split(stage[slot, :, dec_rows : dec_rows + src_rows, :].reshape(-1, jw))
+        coact = dot3(tgts[k], w, src, 1, 0) * norm
+        keep = mask[block, k, :, s_cols(j)]
+        tiles = keep.shape[0]
+        keep = jnp.broadcast_to(keep[:, None, :], (tiles, w // tiles, jw)).reshape(w, jw)
+        weighted = jnp.concatenate(split(virtual * coact * keep), axis=0)
+        evals = split(stage[slot, :, dec_rows + src_rows :, :].reshape(-1, jw))
+        acc[k] += dot3(weighted, w, evals, 1, 1)
 
     def p_copy(k):
         return remote(acc.at[k], arrived.at[k], p_send.at[k], p_recv.at[k], r ^ 2, c)
@@ -331,7 +343,7 @@
 
     def activate(k):
         p_copy(k).wait_recv()
-        column = bias[pl.ds(pl.multiple_of(parity * half + k * w, w), w), :]
+        column = jnp.broadcast_to(bias[pl.ds(parity * T_CHUNKS + k, 1), :], (128, w)).T[:, :1]
         hidden[parity, k] = jnp.maximum((acc[k] + arrived[k]) * scale + column, 0.0)
         h_copy(k, parity).start()
 
@@ -341,15 +353,26 @@
             left = jnp.concatenate(split(decoder[:, t_cols(side, k)]), axis=0)
             recon[...] += dot3(left, decoder.shape[0], split(hidden[side, k]), 1, 0)
 
+    def piece(i):
+        rows = rsend.shape[0] // n_col
+        return pl.ds(pl.multiple_of((c ^ i) * rows, rows), rows)
+
+    def pair_copy(i):
+        return remote(
+            rsend.at[piece(i ^ CORE)], rrecv.at[c ^ i ^ CORE], r_send.at[i ^ CORE], r_recv.at[i ^ CORE], r, c ^ CORE
+        )
+
+    def pair_sum(i):
+        slot = rrecv.at[c ^ i]
+        remote(slot, slot, r_send.at[i ^ CORE], r_recv.at[i ^ CORE], r, c ^ CORE).wait_recv()
+        return rsend[piece(i), :] + rrecv[c ^ i]
+
     def scatter_copy(i):
-        rows = rsend.shape[0] // n_col
-        there = c ^ i
-        return remote(
-            rsend.at[pl.ds(pl.multiple_of(there * rows, rows), rows)], rrecv.at[c], r_send.at[i - 1], r_recv.at[i - 1], r, there
-        )
+        return remote(rsum.at[c ^ i], rlast.at[c], r_send.at[i], r_recv.at[i], r, c ^ i)
 
     def scatter_wait(i):
-        remote(rrecv.at[c ^ i], rrecv.at[c ^ i], r_send.at[i - 1], r_recv.at[i - 1], r, c ^ i).wait_recv()
+        slot = rlast.at[c ^ i]
+        remote(slot, slot, r_send.at[i], r_recv.at[i], r, c ^ i).wait_recv()
 
     barrier = pltpu.get_barrier_semaphore()
     for s in range(1, n_row):
@@ -360,14 +383,14 @@
 
     m_copy().start()
     for s in range(1, n_row):
-        t_copy(0, s).start()
+        t_start(0, s)
     spread(0)
     for j in range(S_CHUNKS):
-        s_copy(j).start()
+        s_start(j)
     spread(1)
     for k in range(1, T_CHUNKS):
         for s in range(1, n_row):
-            t_copy(k, s).start()
+            t_start(k, s)
     own_mask = pltpu.make_async_copy(masks.at[parity], mask.at[0], local_sem.at[n_row])
     own_mask.start()
     own_decoder = pltpu.make_async_copy(dec_tgt, decoder, local_sem.at[n_row + 1])
@@ -435,14 +458,16 @@
             activate(k)
         decode(k)
     rsend[...] = recon[...].T
-    for i in range(1, n_col):
+    chips = (X ^ Y, X, Y)
+    for i in chips + (0,):
+        pair_copy(i).start()
+    for i in chips:
+        rsum[c ^ i] = pair_sum(i)
         scatter_copy(i).start()
-    rows = rsend.shape[0] // n_col
-    for i in range(1, n_col):
+    total = pair_sum(0)
+    for i in chips:
         scatter_wait(i)
-    total = rsend[pl.ds(pl.multiple_of(c * rows, rows), rows), :]
-    for i in range(1, n_col):
-        total = total + rrecv[c ^ i]
+        total = total + rlast[c ^ i]
     out[...] = total
 
     m_copy().wait_send()
@@ -450,13 +475,15 @@
         s_copy(j).wait_send()
     for k in range(T_CHUNKS):
         for s in range(1, n_row):
-            t_copy(k, s).wait_send()
+            t_whole(k, s).wait_send()
         p_copy(k).wait_send()
         h_copy(k, parity).wait_send()
     for q in range(chunks):
         for n in range(len(HOPS)):
             hop(q, n).wait_send()
-    for i in range(1, n_col):
+    for i in chips + (0,):
+        pair_copy(i).wait_send()
+    for i in chips:
         scatter_copy(i).wait_send()
 
 
@@ -467,8 +494,7 @@
     half = features // 2
     w = half // T_CHUNKS
     jw = count // S_CHUNKS
-    packed = jnp.concatenate([dec_src, src_coacts, eval_src], axis=0)
-    blocks = jnp.concatenate([enc_tgt, tgt_coacts], axis=0)
+    packed_rows, block_rows = dec_rows + src_rows + ev_rows, enc_rows + tgt_rows
     tile = count // tile_mask.shape[0]
     masks = jnp.repeat(tile_mask.T.astype(jnp.float32), tile, axis=1).reshape(2, T_CHUNKS, w // tile, count)
     sizes = (
@@ -483,18 +509,18 @@
     hops = (2 * S_CHUNKS, len(HOPS))
     outs = pl.pallas_call(
         functools.partial(fused, sizes),
-        in_specs=[anywhere, anywhere, anywhere, vmem, anywhere],
+        in_specs=[anywhere] * 6 + [vmem, anywhere],
         out_specs=[vmem, anywhere, anywhere],
         out_shape=[
             jax.ShapeDtypeStruct((ev_rows, dec_tgt.shape[0]), f32),
-            jax.ShapeDtypeStruct((2, n_col, packed.shape[0], count), f32),
-            jax.ShapeDtypeStruct((T_CHUNKS, n_row, blocks.shape[0], w), f32),
+            jax.ShapeDtypeStruct((2, n_col, packed_rows, count), f32),
+            jax.ShapeDtypeStruct((T_CHUNKS, n_row, block_rows, w), f32),
         ],
         scratch_shapes=[
-            pltpu.VMEM((n_row, blocks.shape[0], w), f32),
+            pltpu.VMEM((n_row, block_rows, w), f32),
             pltpu.VMEM((T_CHUNKS, 2 * w, depth), bf16),
             pltpu.VMEM((T_CHUNKS, 2 * w, stats), bf16),
-            pltpu.VMEM((2, n_col, packed.shape[0], jw), f32),
+            pltpu.VMEM((2, n_col, packed_rows, jw), f32),
             pltpu.VMEM((2,) + masks.shape[1:], f32),
             pltpu.VMEM((T_CHUNKS, w, evals), f32),
             pltpu.VMEM((T_CHUNKS, w, evals), f32),
@@ -503,19 +529,21 @@
             pltpu.VMEM((dec_tgt.shape[0], evals), f32),
             pltpu.VMEM((evals, dec_tgt.shape[0]), f32),
             pltpu.VMEM((n_col, ev_rows, dec_tgt.shape[0]), f32),
+            pltpu.VMEM((n_col, ev_rows, dec_tgt.shape[0]), f32),
+            pltpu.VMEM((n_col, ev_rows, dec_tgt.shape[0]), f32),
             dma((T_CHUNKS, n_row - 1)), dma((T_CHUNKS, n_row - 1)),
             dma((S_CHUNKS,)), dma((S_CHUNKS,)),
             dma(()), dma(()),
             dma(hops), dma(hops),
             dma((T_CHUNKS,)), dma((T_CHUNKS,)),
             dma((T_CHUNKS,)), dma((T_CHUNKS,)),
-            dma((n_col - 1,)), dma((n_col - 1,)),
+            dma((n_col,)), dma((n_col,)),
             dma((n_row + 2,)), dma((2, n_col)),
         ],
         compiler_params=pltpu.CompilerParams(
             collective_id=0, has_side_effects=True, vmem_limit_bytes=VMEM_LIMIT
         ),
-    )(packed, blocks, masks, enc_bias.reshape(-1, 1), dec_tgt)
+    )(dec_src, src_coacts, eval_src, enc_tgt, tgt_coacts, masks, enc_bias.reshape(-1, w), dec_tgt)
     return outs[0]
 
 

time: 436 us -> 399 us (0.915); the launches traced: 436 us -> 392 us
  Pallas kernels: 423 us -> 388 us
  other arithmetic: 8.2 us -> 0.72 us
    pallas_call x1, Pallas kernels: 423 us -> 388 us  [whole(): pl.pallas_call(functools.partial(fused, sizes), in_specs=[anywhere] * 6 +...]
    concatenate x2 -> x0, other arithmetic: 7.39 us -> none  [the longest x1 4.24 us: whole(): packed = jnp.concatenate([dec_src, src_coacts, eval_src], axis=0)]
where the time goes in v1:
time: 399 us; the launch traced here: 392 us
  Pallas kernels  388 us (97%)
  local copies, waits for them, and re-layouts  4.1 us (1%)
    pallas_call x1, Pallas kernels, whole(): pl.pallas_call(functools.partial(fused, sizes), in_specs=[anywhere] * 6 +...  388 us

profile of v1, /device:TPU:9, one launch (start us, length us, event | category | flops | bytes accessed | tf_op | source)
XLA Modules:
  0.0 392.4 jit_solution(3850760878009653132)
XLA Ops:
  0.0 1.3 reshape.3.bias
  1.3 0.7 convert_bitcast_fusion
  2.0 0.1 copy.9
  2.1 0.2 broadcast_in_dim.3
  2.3 0.9 reshape_reshape.3.masks
  3.2 387.6 %shard_map.82 = (f32[64,576]{1,0:T(8,128)}, f32[2,8,416,2048]{3,2,1,0:T(8,128)}, f32[4,4,704,256]{3,2,1,0:T(8,128)}) custom-call(f32[288,2048]{1,0:T(8,128)} %dec_src.1, f32[64,2048]{1,0:T(8,128)} %src_coacts.1, f32[64,2048]{1,0:T(8,128)} %eval_src.1, f32[576,2048]{1,0:T(8,128)} %enc_tgt.1, f32[128,2048]{1,0:T(8,128)} %tgt_coacts.1, ...), custom_call_target="tpu_custom_call" | custom-call | tf_op jit(solution)/shard_map/pallas_call | solution.py:510
  390.9 1.6 copy.11

commit v2 on v1

--- a/solution.py
+++ b/solution.py
@@ -165,6 +165,7 @@
 MESH = pl.DeviceIdType.MESH
 T_CHUNKS = 4
 S_CHUNKS = 4
+BANDS = 2
 X, Y, CORE = 2, 4, 1
 HOPS = (
     (0, "all", X), (0, "all", Y), (0, "all", CORE),
@@ -335,23 +336,27 @@
         evals = split(stage[slot, :, dec_rows + src_rows :, :].reshape(-1, jw))
         acc[k] += dot3(weighted, w, evals, 1, 1)
 
-    def p_copy(k):
-        return remote(acc.at[k], arrived.at[k], p_send.at[k], p_recv.at[k], r ^ 2, c)
-
-    def h_copy(k, side):
-        return remote(hidden.at[side, k], hidden.at[side, k], h_send.at[k], h_recv.at[k], r ^ 1, c)
+    def bands():
+        return [(b, pl.ds(b * (w // BANDS), w // BANDS)) for b in range(BANDS)]
+
+    def p_copy(k, b, rows):
+        return remote(acc.at[k, rows], arrived.at[k, rows], p_send.at[k, b], p_recv.at[k, b], r ^ 2, c)
+
+    def h_copy(k, b, rows, side):
+        part = hidden.at[side, k, rows]
+        return remote(part, part, h_send.at[k, b], h_recv.at[k, b], r ^ 1, c)
 
     def activate(k):
-        p_copy(k).wait_recv()
         column = jnp.broadcast_to(bias[pl.ds(parity * T_CHUNKS + k, 1), :], (128, w)).T[:, :1]
-        hidden[parity, k] = jnp.maximum((acc[k] + arrived[k]) * scale + column, 0.0)
-        h_copy(k, parity).start()
-
-    def decode(k):
-        h_copy(k, 1 - parity).wait_recv()
-        for side in range(2):
-            left = jnp.concatenate(split(decoder[:, t_cols(side, k)]), axis=0)
-            recon[...] += dot3(left, decoder.shape[0], split(hidden[side, k]), 1, 0)
+        for b, rows in bands():
+            p_copy(k, b, rows).wait_recv()
+            total = (acc[k, rows, :] + arrived[k, rows, :]) * scale + column[b * (w // BANDS) : (b + 1) * (w // BANDS)]
+            hidden[parity, k, rows, :] = jnp.maximum(total, 0.0)
+            h_copy(k, b, rows, parity).start()
+
+    def decode(k, side):
+        left = jnp.concatenate(split(decoder[:, t_cols(side, k)]), axis=0)
+        recon[...] += dot3(left, decoder.shape[0], split(hidden[side, k]), 1, 0)
 
     def piece(i):
         rows = rsend.shape[0] // n_col
@@ -447,16 +452,28 @@
 
         @pl.when((g == 14) | (g == 15) | (g == 23) | (g == 31))
         def _():
-            p_copy(k).start()
+            for b, rows in bands():
+                p_copy(k, b, rows).start()
 
         @pl.when((g == 27) | (g == 28) | (g == 30))
         def _():
             activate(jnp.where(g == 30, 2, g - 27))
 
-    for k in range(T_CHUNKS):
-        if k == T_CHUNKS - 1:
-            activate(k)
-        decode(k)
+    last = T_CHUNKS - 1
+
+    @pl.loop(0, last)
+    def _(k):
+        decode(k, parity)
+
+    activate(last)
+    decode(last, parity)
+
+    @pl.loop(0, T_CHUNKS)
+    def _(k):
+        for b, rows in bands():
+            h_copy(k, b, rows, 1 - parity).wait_recv()
+        decode(k, 1 - parity)
+
     rsend[...] = recon[...].T
     chips = (X ^ Y, X, Y)
     for i in chips + (0,):
@@ -476,8 +493,9 @@
     for k in range(T_CHUNKS):
         for s in range(1, n_row):
             t_whole(k, s).wait_send()
-        p_copy(k).wait_send()
-        h_copy(k, parity).wait_send()
+        for b, rows in bands():
+            p_copy(k, b, rows).wait_send()
+            h_copy(k, b, rows, parity).wait_send()
     for q in range(chunks):
         for n in range(len(HOPS)):
             hop(q, n).wait_send()
@@ -535,8 +553,8 @@
             dma((S_CHUNKS,)), dma((S_CHUNKS,)),
             dma(()), dma(()),
             dma(hops), dma(hops),
-            dma((T_CHUNKS,)), dma((T_CHUNKS,)),
-            dma((T_CHUNKS,)), dma((T_CHUNKS,)),
+            dma((T_CHUNKS, BANDS)), dma((T_CHUNKS, BANDS)),
+            dma((T_CHUNKS, BANDS)), dma((T_CHUNKS, BANDS)),
             dma((n_col,)), dma((n_col,)),
             dma((n_row + 2,)), dma((2, n_col)),
         ],

time: 399 us -> 394 us (0.987); the launches traced: 392 us -> 392 us
  no operation moved by 1% of the time
where the time goes in v2:
time: 394 us; the launch traced here: 392 us
  Pallas kernels  387 us (98%)
  local copies, waits for them, and re-layouts  4.1 us (1%)
    pallas_call x1, Pallas kernels, whole(): pl.pallas_call(functools.partial(fused, sizes), in_specs=[anywhere] * 6 +...  387 us

profile of v2, /device:TPU:9, one launch (start us, length us, event | category | flops | bytes accessed | tf_op | source)
XLA Modules:
  0.0 392.3 jit_solution(9746337420979265756)
XLA Ops:
  0.0 1.3 reshape.3.bias
  1.3 0.7 convert_bitcast_fusion
  2.0 0.1 copy.9
  2.1 0.2 broadcast_in_dim.3
  2.3 0.9 reshape_reshape.3.masks
  3.2 387.5 %shard_map.82 = (f32[64,576]{1,0:T(8,128)}, f32[2,8,416,2048]{3,2,1,0:T(8,128)}, f32[4,4,704,256]{3,2,1,0:T(8,128)}) custom-call(f32[288,2048]{1,0:T(8,128)} %dec_src.1, f32[64,2048]{1,0:T(8,128)} %src_coacts.1, f32[64,2048]{1,0:T(8,128)} %eval_src.1, f32[576,2048]{1,0:T(8,128)} %enc_tgt.1, f32[128,2048]{1,0:T(8,128)} %tgt_coacts.1, ...), custom_call_target="tpu_custom_call" | custom-call | tf_op jit(solution)/shard_map/pallas_call | solution.py:528
  390.7 1.6 copy.11
